TPU v7x, 32 devices: a whole 2x2x4 slice. The times are simulated.
32 devices in a mesh: dp: 8 (over z, y), tensor: 4 (over x, core).
Axes of the slice: x: 2, y: 2, z: 4, core: 2. Of those that a mesh axis runs over, the one named last changes fastest.
Arguments:
- tokens: bfloat16 [8, 512, 768], P('dp'), as said below
- cotangent: bfloat16 [8, 512, 768], P('dp'), may hold values from -6 to 6
- lengths: int32 [8], P('dp'), may hold values from 128 to 512, as said below
- in_weight: float32 [7, 768, 768], P(None, 'dp', 'tensor'), as said below
- out_weight: float32 [5, 768, 768], P(None, 'tensor', 'dp'), may hold values from -0.4375 to 0.4375
- in_bias: float32 [6, 768], P(None, 'tensor'), may hold values from -3 to 3
- norm_vec: float32 [6, 768], replicated, may hold values from 0.1 to 1.9
- in_moments: float32 [2, 7, 768, 768], P(None, None, 'dp', 'tensor'), as said below
- out_moments: float32 [2, 5, 768, 768], P(None, None, 'tensor', 'dp'), as said below
- bias_moments: float32 [2, 6, 768], P(None, None, 'tensor'), as said below
- norm_moments: float32 [2, 6, 768], replicated, as said below
Outputs:
- output: bfloat16 [8, 512, 768], P('dp')
- grad_input: bfloat16 [8, 512, 768], P('dp')
- in_grad: float32 [7, 768, 768], P(None, 'dp', 'tensor')
- out_grad: float32 [5, 768, 768], P(None, 'tensor', 'dp')
- bias_grad: float32 [6, 768], P(None, 'tensor')
- norm_grad: float32 [6, 768], replicated
- new_in_weight: float32 [7, 768, 768], P(None, 'dp', 'tensor')
- new_out_weight: float32 [5, 768, 768], P(None, 'tensor', 'dp')
- new_in_bias: float32 [6, 768], P(None, 'tensor')
- new_norm_vec: float32 [6, 768], replicated
- new_in_moments: float32 [2, 7, 768, 768], P(None, None, 'dp', 'tensor')
- new_out_moments: float32 [2, 5, 768, 768], P(None, None, 'tensor', 'dp')
- new_bias_moments: float32 [2, 6, 768], P(None, None, 'tensor')
- new_norm_moments: float32 [2, 6, 768], replicated
Inputs may be any that keep to these rules, and one draw needn't show every extreme that they name: `lengths`: each sequence's live tokens come first; the first sequence is full, with 512 live tokens. `tokens`: entries lie within -6 and 6. `in_weight`: entries lie within -6 / sqrt(768) and 6 / sqrt(768). `in_moments`: second moments (index 1) are positive. `out_moments`: second moments (index 1) are positive. `bias_moments`: second moments (index 1) are positive. `norm_moments`: second moments (index 1) are positive.
All inputs are finite; a program needn't handle non-finite values.
Results may differ from a plain program's by a relative error of at most 0.023.
Values may be sent and summed in bfloat16 or wider, within the bound.
A program may use at most 128 MiB of HBM per device.

v0:
```python
import jax
import jax.numpy as jnp
from jax import lax
from jax.sharding import PartitionSpec as P

HDIM = 64
norm_eps = 1e-12
masked_score = -1e30
learn_rate = 0.005
beta_first = 0.9
beta_second = 0.999
adam_eps = 1e-08
weight_decay = 0.01
step_count = 2.0
root_half = 0.7071067811865476
normal_peak = 0.3989422804014327


def matmul(left_op, right_op):
    return jnp.dot(left_op, right_op, preferred_element_type=jnp.float32)


def inner_rows(left_op, right_op):
    return lax.dot_general(
        left_op, right_op, (((0,), (0,)), ((), ())), preferred_element_type=jnp.float32
    )


def times_transposed(left_op, right_op):
    return lax.dot_general(
        left_op, right_op, (((1,), (1,)), ((), ())), preferred_element_type=jnp.float32
    )


def layer_norm(summed_rows, gain_vec, shift_vec):
    center = jnp.mean(summed_rows, -1, keepdims=True)
    offset = summed_rows - center
    inverse = lax.rsqrt(jnp.mean(offset * offset, -1, keepdims=True) + norm_eps)
    normed = offset * inverse
    return (normed * gain_vec + shift_vec, normed, inverse)


def norm_back(upstream, normed, inverse, gain_vec):
    scaled = upstream * gain_vec
    return inverse * (
        scaled
        - jnp.mean(scaled, -1, keepdims=True)
        - normed * jnp.mean(scaled * normed, -1, keepdims=True)
    )


def gelu_value(pre_act):
    return 0.5 * pre_act * (1.0 + jax.scipy.special.erf(pre_act * root_half))


def gelu_slope(pre_act):
    return (
        0.5 * (1.0 + jax.scipy.special.erf(pre_act * root_half))
        + pre_act * jnp.exp(-0.5 * pre_act * pre_act) * normal_peak
    )


def score_block(query_heads, key_heads, length):
    seq_len = query_heads.shape[0]
    scale_factor = query_heads.shape[-1] ** (-0.5)
    scores = (
        jnp.einsum("qhe,khe->hqk", query_heads, key_heads, preferred_element_type=jnp.float32)
        * scale_factor
    )
    usable = lax.broadcasted_iota(jnp.int32, (1, 1, seq_len), 2) < length
    return jnp.where(usable, scores, masked_score)


def attend_forward(operands):
    query_heads, key_heads, value_heads, length = operands
    scores = score_block(query_heads, key_heads, length)
    highest = jnp.max(scores, -1, keepdims=True)
    log_total = highest + jnp.log(jnp.sum(jnp.exp(scores - highest), -1, keepdims=True))
    probs_low = jnp.exp(scores - log_total).astype(jnp.bfloat16)
    mixed_heads = jnp.einsum(
        "hqk,khe->qhe", probs_low, value_heads, preferred_element_type=jnp.float32
    )
    return (mixed_heads.astype(jnp.bfloat16), log_total)


def attend_backward(operands):
    query_heads, key_heads, value_heads, grad_heads, log_total, length = operands
    scale_factor = query_heads.shape[-1] ** (-0.5)
    scores = score_block(query_heads, key_heads, length)
    probs = jnp.exp(scores - log_total)
    probs_low = probs.astype(jnp.bfloat16)
    grad_probs = jnp.einsum(
        "qhe,khe->hqk", grad_heads, value_heads, preferred_element_type=jnp.float32
    )
    row_dot = jnp.sum(probs * grad_probs, -1, keepdims=True)
    grad_scores = (probs * (grad_probs - row_dot) * scale_factor).astype(jnp.bfloat16)
    grad_query = jnp.einsum(
        "hqk,khe->qhe", grad_scores, key_heads, preferred_element_type=jnp.float32
    )
    grad_keys = jnp.einsum(
        "hqk,qhe->khe", grad_scores, query_heads, preferred_element_type=jnp.float32
    )
    grad_values = jnp.einsum(
        "hqk,qhe->khe", probs_low, grad_heads, preferred_element_type=jnp.float32
    )
    return (grad_query, grad_keys, grad_values)


def adam_update(param, grad, moments, decay):
    first = beta_first * moments[0] + (1.0 - beta_first) * grad
    second = beta_second * moments[1] + (1.0 - beta_second) * grad * grad
    first_hat = first / (1.0 - beta_first**step_count)
    second_hat = second / (1.0 - beta_second**step_count)
    new_param = param - learn_rate * (first_hat / (jnp.sqrt(second_hat) + adam_eps) + decay * param)
    return (new_param, jnp.stack([first, second]))


def local(
    tokens,
    cotangent,
    lengths,
    in_weight,
    out_weight,
    in_bias,
    norm_vec,
    in_moments,
    out_moments,
    bias_moments,
    norm_moments,
):
    seq_count, seq_len, width = tokens.shape
    row_count = seq_count * seq_len
    in_full, out_full = (
        lax.all_gather(in_weight.astype(jnp.bfloat16), "dp", axis=1, tiled=True),
        lax.all_gather(out_weight.astype(jnp.bfloat16), "dp", axis=2, tiled=True),
    )
    group_width = in_full.shape[2]
    heads_here = group_width // HDIM
    w_query, w_key, w_value = (in_full[0], in_full[1], in_full[2])
    w_up = in_full[3:7]
    w_proj = out_full[0]
    w_down = out_full[1:5]
    bias_up = in_bias[2:6]

    def split_heads(flat_rows):
        return flat_rows.reshape(seq_count, seq_len, heads_here, HDIM)

    flat_tokens = tokens.reshape(row_count, width)
    query = (matmul(flat_tokens, w_query) + in_bias[0]).astype(jnp.bfloat16)
    keys_low = matmul(flat_tokens, w_key).astype(jnp.bfloat16)
    values_low = (matmul(flat_tokens, w_value) + in_bias[1]).astype(jnp.bfloat16)
    mixed_heads, log_total = lax.map(
        attend_forward,
        (split_heads(query), split_heads(keys_low), split_heads(values_low), lengths),
    )
    mixed_flat = mixed_heads.reshape(row_count, group_width)
    attn_out = lax.psum(matmul(mixed_flat, w_proj).astype(jnp.bfloat16), "tensor").astype(
        jnp.float32
    )
    hidden, normed_one, inverse_one = layer_norm(
        flat_tokens.astype(jnp.float32) + attn_out + norm_vec[0], norm_vec[1], norm_vec[2]
    )
    hidden_low = hidden.astype(jnp.bfloat16)
    pre_act = (
        jnp.einsum("rd,kdj->rkj", hidden_low, w_up, preferred_element_type=jnp.float32) + bias_up
    )
    act_low = gelu_value(pre_act).astype(jnp.bfloat16)
    ffn_part = jnp.einsum("rkj,kjd->rd", act_low, w_down, preferred_element_type=jnp.float32)
    ffn_out = lax.psum(ffn_part.astype(jnp.bfloat16), "tensor").astype(jnp.float32)
    out_rows, normed_two, inverse_two = layer_norm(
        hidden + ffn_out + norm_vec[3], norm_vec[4], norm_vec[5]
    )
    positions = lax.broadcasted_iota(jnp.int32, (seq_count, seq_len), 1)
    live_rows = (positions < lengths[:, None]).astype(jnp.float32).reshape(row_count, 1)
    grad_out = cotangent.reshape(row_count, width).astype(jnp.float32) * live_rows
    grad_two = norm_back(grad_out, normed_two, inverse_two, norm_vec[4])
    grad_two_low = grad_two.astype(jnp.bfloat16)
    grad_down = jnp.einsum("rkj,rd->kjd", act_low, grad_two_low, preferred_element_type=jnp.float32)
    grad_act = jnp.einsum("rd,kjd->rkj", grad_two_low, w_down, preferred_element_type=jnp.float32)
    grad_pre = grad_act * gelu_slope(pre_act)
    grad_pre_low = grad_pre.astype(jnp.bfloat16)
    grad_up = jnp.einsum(
        "rd,rkj->kdj", hidden_low, grad_pre_low, preferred_element_type=jnp.float32
    )
    back_part = jnp.einsum("rkj,kdj->rd", grad_pre_low, w_up, preferred_element_type=jnp.float32)
    grad_hidden = grad_two + lax.psum(back_part.astype(jnp.bfloat16), "tensor").astype(jnp.float32)
    grad_one = norm_back(grad_hidden, normed_one, inverse_one, norm_vec[1])
    grad_one_low = grad_one.astype(jnp.bfloat16)
    grad_proj = inner_rows(mixed_flat, grad_one_low)
    grad_mixed = times_transposed(grad_one_low, w_proj).astype(jnp.bfloat16)
    grad_query, grad_keys, grad_values = lax.map(
        attend_backward,
        (
            split_heads(query),
            split_heads(keys_low),
            split_heads(values_low),
            split_heads(grad_mixed),
            log_total,
            lengths,
        ),
    )
    grad_query = grad_query.reshape(row_count, group_width)
    grad_keys = grad_keys.reshape(row_count, group_width)
    grad_values = grad_values.reshape(row_count, group_width)
    query_grad_low = grad_query.astype(jnp.bfloat16)
    keys_grad_low = grad_keys.astype(jnp.bfloat16)
    values_grad_low = grad_values.astype(jnp.bfloat16)
    input_part = (
        times_transposed(query_grad_low, w_query)
        + times_transposed(keys_grad_low, w_key)
        + times_transposed(values_grad_low, w_value)
    )
    grad_input = grad_one + lax.psum(input_part.astype(jnp.bfloat16), "tensor").astype(jnp.float32)
    grad_in = jnp.concatenate(
        [
            jnp.stack(
                [
                    inner_rows(flat_tokens, query_grad_low),
                    inner_rows(flat_tokens, keys_grad_low),
                    inner_rows(flat_tokens, values_grad_low),
                ]
            ),
            grad_up,
        ],
        0,
    )
    grad_outw = jnp.concatenate([grad_proj[None], grad_down], 0)
    grad_bias = jnp.concatenate(
        [jnp.stack([jnp.sum(grad_query, 0), jnp.sum(grad_values, 0)]), jnp.sum(grad_pre, 0)], 0
    )
    grad_norm = jnp.stack(
        [
            jnp.sum(grad_one, 0),
            jnp.sum(grad_hidden * normed_one, 0),
            jnp.sum(grad_hidden, 0),
            jnp.sum(grad_two, 0),
            jnp.sum(grad_out * normed_two, 0),
            jnp.sum(grad_out, 0),
        ]
    )
    in_total, out_total, bias_total, norm_total = lax.psum(
        (grad_in, grad_outw, grad_bias, grad_norm), "dp"
    )
    owner = lax.axis_index("dp")
    in_rows = in_weight.shape[1]
    out_cols = out_weight.shape[2]
    in_share = lax.dynamic_slice_in_dim(in_total, owner * in_rows, in_rows, 1)
    out_share = lax.dynamic_slice_in_dim(out_total, owner * out_cols, out_cols, 2)
    new_in_weight, new_in_moments = adam_update(in_weight, in_share, in_moments, weight_decay)
    new_out_weight, new_out_moments = adam_update(out_weight, out_share, out_moments, weight_decay)
    new_in_bias, new_bias_moments = adam_update(in_bias, bias_total, bias_moments, 0.0)
    new_norm_vec, new_norm_moments = adam_update(norm_vec, norm_total, norm_moments, 0.0)
    output = out_rows.astype(jnp.bfloat16).reshape(seq_count, seq_len, width)
    grad_tokens = grad_input.astype(jnp.bfloat16).reshape(seq_count, seq_len, width)
    return (
        output,
        grad_tokens,
        in_share,
        out_share,
        bias_total,
        norm_total,
        new_in_weight,
        new_out_weight,
        new_in_bias,
        new_norm_vec,
        new_in_moments,
        new_out_moments,
        new_bias_moments,
        new_norm_moments,
    )


def solution(mesh):
    in_specs = (
        P("dp", None, None),
        P("dp", None, None),
        P("dp"),
        P(None, "dp", "tensor"),
        P(None, "tensor", "dp"),
        P(None, "tensor"),
        P(),
        P(None, None, "dp", "tensor"),
        P(None, None, "tensor", "dp"),
        P(None, None, "tensor"),
        P(),
    )
    out_specs = (
        P("dp", None, None),
        P("dp", None, None),
        P(None, "dp", "tensor"),
        P(None, "tensor", "dp"),
        P(None, "tensor"),
        P(),
        P(None, "dp", "tensor"),
        P(None, "tensor", "dp"),
        P(None, "tensor"),
        P(),
        P(None, None, "dp", "tensor"),
        P(None, None, "tensor", "dp"),
        P(None, None, "tensor"),
        P(),
    )
    return jax.shard_map(local, mesh=mesh, in_specs=in_specs, out_specs=out_specs, check_vma=False)
```

profile of v0, /device:TPU:0, one launch (start us, length us, event | category | flops | bytes accessed | tf_op | source)
XLA Modules:
  0.0 594.2 jit_solution(6022142361547197899)
XLA Ops:
  11.3 62.3 %all-gather.5.cloned.1.call-done = bf16[5,192,768]{1,0,2:T(8,128)(2,1)} async-done(((bf16[5,192,96]{1,0,2:T(8,128)(2,1)}), bf16[5,192,768]{1,0,2:T(8,128)(2,1)}) %all-gather.5.cloned.1.call-update) | async-done | bytes 1474576 | tf_op jit(solution)/shard_map/all_gather | solution.py:135
  73.5 2.4 slice.97
  76.0 1.6 copy.139
  77.6 57.4 %all-gather.3.cloned.1.call-done = bf16[7,768,192]{2,0,1:T(8,128)(2,1)} async-done(((bf16[7,96,192]{2,0,1:T(8,128)(2,1)}), bf16[7,768,192]{2,0,1:T(8,128)(2,1)}) %all-gather.3.cloned.1.call-update) | async-done | bytes 2064400 | tf_op jit(solution)/shard_map/all_gather | solution.py:134
  135.0 6.1 %fusion.97 = (bf16[1,768,192]{2,0,1:T(2,128)(2,1)S(1)}, bf16[1,768,192]{2,0,1:T(2,128)(2,1)S(1)}, bf16[1,768,192]{2,0,1:T(2,128)(2,1)S(1)}) fusion(bf16[7,768,192]{2,0,1:T(8,128)(2,1)} %all-gather.3.cloned.1.call-done), kind=kLoop, calls=%fused_computation.162 | loop fusion | bytes 1769472 | tf_op jit(solution)/shard_map/slice | solution.py:139
  141.2 1.6 copy.136
  148.1 1.3 convolution_convert_fusion
  149.5 2.8 slice.99
  152.3 2.2 copy.141
  154.5 2.7 slice.98
  157.2 2.1 copy.140
  159.4 23.8 %all-reduce.8.cloned.1.call-done = bf16[512,768]{1,0:T(8,128)(2,1)} async-done(((bf16[512,768]{1,0:T(8,128)(2,1)}), bf16[512,768]{1,0:T(8,128)(2,1)}) %all-reduce.8.cloned.1.call-update) | async-done | bytes 786448 | tf_op jit(solution)/shard_map/psum | solution.py:157
  183.2 1.6 fusion.32
  186.4 1.1 copy-done.20
  188.2 1.7 bitcast_convert_fusion.1
  190.2 34.9 %all-reduce.10.cloned.1.call-done = bf16[512,768]{1,0:T(8,128)(2,1)} async-done(((bf16[512,768]{1,0:T(8,128)(2,1)}), bf16[512,768]{1,0:T(8,128)(2,1)}) %all-reduce.10.cloned.1.call-update) | async-done | bytes 786448 | tf_op jit(solution)/shard_map/psum | solution.py:169
  225.1 1.9 fusion.96
  229.1 1.6 fusion.23
  231.1 2.0 fusion.106
  233.9 1.7 bitcast_convert_fusion
  235.7 3.4 fusion.41
  239.1 2.5 convolution_bitcast_fusion
  241.6 29.2 %all-reduce.12.cloned.1.call-done = bf16[512,768]{1,0:T(8,128)(2,1)} async-done(((bf16[512,768]{1,0:T(8,128)(2,1)}), bf16[512,768]{1,0:T(8,128)(2,1)}) %all-reduce.12.cloned.1.call-update) | async-done | bytes 786448 | tf_op jit(solution)/shard_map/psum | solution.py:186
  270.9 2.8 multiply_reduce_fusion.1
  273.7 2.8 fusion.95
  277.5 2.4 fusion.107
  279.8 7.2 %fusion.99 = (f32[3,64]{1,0:T(4,128)}, bf16[512,3,64]{0,2,1:T(8,128)(2,1)S(1)}) fusion(bf16[512,3,64]{0,2,1:T(8,128)(2,1)S(1)} %bitcast.222, f32[3,512,512]{1,2,0:T(8,128)} %fusion.107, f32[3,512]{1,0:T(4,128)S(1)} %log_add_fusion, f32[3,512,512]{1,2,0:T(8,128)} %copy-done.3, pred[512]{0:T(512)(128)(4,1)S(1)} %iota_compare_fusion), kind=kOutput, calls=%fused_computation.164 | convolution fusion | flops 109512512 | bytes 6692096 | tf_op jit(solution)/shard_map/while/body/eval_jaxpr/hqk,khe->qhe/dot_general | solution.py:97
  287.0 6.6 %fusion.35 = bf16[3,64,512]{2,1,0:T(8,128)(2,1)S(1)} fusion(bf16[512,3,64]{0,2,1:T(8,128)(2,1)S(1)} %bitcast.232, f32[3,512,512]{1,2,0:T(8,128)} %fusion.107, f32[3,512,512]{1,2,0:T(8,128)} %copy-done.3, f32[3,512]{1,0:T(4,128)S(1)} %log_add_fusion, pred[512]{0:T(512)(128)(4,1)S(1)} %iota_compare_fusion), kind=kOutput, calls=%fused_computation.65 | convolution fusion | flops 109414400 | bytes 6691328 | tf_op jit(solution)/shard_map/while/body/eval_jaxpr/hqk,qhe->khe/dot_general | solution.py:100
  293.7 3.5 fusion.100
  297.6 1.3 convolution_bitcast_fusion.3
  299.3 1.3 convolution_bitcast_fusion.4
  300.6 1.1 convolution_bitcast_fusion.1
  301.7 1.1 convolution_bitcast_fusion.2
  302.9 1.3 add_convert_fusion.1
  304.3 3.8 pad_maximum_fusion.1
  308.1 2.3 pad_maximum_fusion
  312.6 2.3 fusion.98
  314.9 1.5 copy.142
  318.0 37.5 %all-reduce = (f32[6,192]{1,0:T(8,128)S(1)}, f32[6,768]{1,0:T(8,128)S(1)}) all-reduce(f32[6,192]{1,0:T(8,128)S(1)} %pad_maximum_fusion.6, f32[6,768]{1,0:T(8,128)S(1)} %stack.83), channel_id=1, replica_groups=mesh['dp'=8,'tensor'=4] {'dp'}, use_global_device_ids=true, to_apply=%region_20.21 | all-reduce | flops 5760 | bytes 46080 | tf_op jit(solution)/shard_map/psum | solution.py:241
  358.0 2.2 fusion.39
  360.2 214.8 %all-reduce.16.cloned.1.call-done = (f32[7,768,192]{1,2,0:T(8,128)}, f32[5,192,768]{2,1,0:T(8,128)}) async-done(((f32[7,768,192]{1,2,0:T(8,128)}, f32[5,192,768]{2,1,0:T(8,128)}), (f32[7,768,192]{1,2,0:T(8,128)}, f32[5,192,768]{2,1,0:T(8,128)})) %all-reduce.16.cloned.1.call-update) | async-done | bytes 7077904 | tf_op jit(solution)/shard_map/psum | solution.py:241
  575.0 1.7 fusion.70
  576.7 1.1 copy.127
  577.8 1.6 fusion.74
  579.4 2.4 copy.128
  581.8 1.4 fusion.75
  583.2 1.3 fusion.76
  584.7 1.6 copy.129
  (181 shorter events, 23.7 us)
Async XLA Ops:
  7.2 2.3 copy-start.7
  7.2 66.3 %all-gather.5.cloned.1.call-start = ((), (), s32[]{:S(2)}) async-start(), calls=%async_computation.1 | async-start | bytes 3538944 | tf_op jit(solution)/shard_map/all_gather | solution.py:135
  8.4 2.9 copy-start.43
  9.5 125.5 %all-gather.3.cloned.1.call-start = ((), (), s32[]{:S(2)}) async-start(), calls=%async_computation | async-start | bytes 3538944 | tf_op jit(solution)/shard_map/all_gather | solution.py:134
  10.5 172.7 %all-reduce.8.cloned.1.call-start = ((), (), s32[]{:S(2)}) async-start(), calls=%async_computation.2 | async-start | bytes 1572864 | tf_op jit(solution)/shard_map/psum | solution.py:157
  141.1 2.6 copy-start
  145.4 1.6 copy-start.3
  149.4 75.7 %all-reduce.10.cloned.1.call-start = ((), (), s32[]{:S(2)}) async-start(), calls=%async_computation.3 | async-start | bytes 1572864 | tf_op jit(solution)/shard_map/psum | solution.py:169
  183.2 1.6 copy-start.2
  183.2 2.1 copy-start.26
  186.4 1.8 copy-start.24
  188.2 1.7 copy-start.4
  189.9 80.9 %all-reduce.12.cloned.1.call-start = ((), (), s32[]{:S(2)}) async-start(), calls=%async_computation.4 | async-start | bytes 1572864 | tf_op jit(solution)/shard_map/psum | solution.py:186
  229.1 1.6 copy-start.21
  229.1 2.0 copy-start.25
  230.6 40.2 %copy-start.1 = (f32[512,768]{1,0:T(8,128)}, f32[512,768]{1,0:T(8,128)S(1)}, u32[]{:S(2)}) copy-start(f32[512,768]{1,0:T(8,128)S(1)} %get-tuple-element.165) | copy-start | bytes 4718596
  231.1 2.9 copy-start.27
  235.7 122.3 %all-reduce.14.cloned.1.call-start = ((), (), s32[]{:S(2)}) async-start(), calls=%async_computation.5 | async-start | bytes 1572864 | tf_op jit(solution)/shard_map/psum | solution.py:213
  235.7 3.4 copy-start.55
  270.9 2.8 copy-start.5
  273.7 2.8 copy-start.13
  277.5 2.4 copy-start.33
  279.8 7.2 %copy-start.39 = (bf16[512,192]{0,1:T(8,128)(2,1)S(1)}, bf16[512,192]{0,1:T(8,128)(2,1)}, u32[]{:S(2)}) copy-start(bf16[512,192]{0,1:T(8,128)(2,1)} %copy-done.38) | copy-start | bytes 589828
  287.0 11.8 %copy-start.34 = (bf16[512,3,64]{0,2,1:T(8,128)(2,1)}, bf16[512,3,64]{0,2,1:T(8,128)(2,1)S(1)}, u32[]{:S(2)}) copy-start(bf16[512,3,64]{0,2,1:T(8,128)(2,1)S(1)} %get-tuple-element.174) | copy-start | bytes 589828
  293.7 3.5 copy-start.35
  297.2 1.7 copy-start.29
  298.9 1.7 copy-start.31
  300.6 2.3 copy-start.23
  304.2 3.9 copy-start.14
  304.2 270.8 %all-reduce.16.cloned.1.call-start = ((), (), s32[]{:S(2)}) async-start(), calls=%async_computation.6 | async-start | bytes 14155776 | tf_op jit(solution)/shard_map/psum | solution.py:241
  304.2 3.8 copy-start.15
  314.9 2.7 copy-start.49
  314.9 2.7 copy-start.42
  314.9 2.8 copy-start.53
  314.9 2.9 copy-start.52
  314.9 2.9 copy-start.48
  314.9 2.9 copy-start.47
  314.9 2.9 copy-start.46
  314.9 2.9 copy-start.45
  314.9 3.0 copy-start.51
  314.9 41.8 %copy-start.41 = (f32[6,768]{1,0:T(8,128)S(1)}, f32[6,768]{1,0:T(8,128)}, u32[]{:S(2)}) copy-start(f32[6,768]{1,0:T(8,128)} %param.17) | copy-start | bytes 55300
  355.5 4.7 copy-start.44
  355.5 4.7 copy-start.50
  575.0 2.9 copy-start.9
  575.0 2.9 copy-start.10
  579.4 2.4 copy-start.16
  579.4 3.8 copy-start.17
  584.7 1.6 copy-start.19
  (15 other events, 17.5 us)
Sparse Core Ops, SparseCore 0:
  10.8 62.7 all-gather.4
  76.3 58.6 all-gather.2
  149.5 33.6 all-reduce.7
  190.0 35.0 all-reduce.9
  235.8 35.0 all-reduce.11
  304.3 35.0 all-reduce.13
  343.4 231.5 all-reduce.15
where the time goes:
time: 595 us; the launch traced here: 594 us
  waiting for transfers between devices  423 us (71%)
  matrix products  43.5 us (7%)
  local copies, waits for them, and re-layouts  43.2 us (7%)
  blocking collectives  37.5 us (6%)
  other arithmetic  31.4 us (5%)
  between operations  15.5 us (3%)
    psum x1, waiting for transfers between devices, local(): lax.psum((grad_in, grad_outw, grad_bias, grad_norm), 'dp')  215 us
    all_gather x1, waiting for transfers between devices, local(): lax.all_gather(out_weight.astype(jnp.bfloat16), 'dp', axis=2, tiled=True)  62.3 us
    all_gather x1, waiting for transfers between devices, local(): lax.all_gather(in_weight.astype(jnp.bfloat16), 'dp', axis=1, tiled=True)  57.4 us
    psum x1, blocking collectives, local(): lax.psum((grad_in, grad_outw, grad_bias, grad_norm), 'dp')  37.5 us
    psum x1, waiting for transfers between devices, local(): lax.psum(ffn_part.astype(jnp.bfloat16), 'tensor').astype(jnp.float32)  34.9 us
    psum x1, waiting for transfers between devices, local(): lax.psum(back_part.astype(jnp.bfloat16), 'tensor').astype(jnp.float32)  29.2 us
    unnamed x126, local copies, waits for them, and re-layouts  24.5 us
    psum x1, waiting for transfers between devices, local(): lax.psum(matmul(mixed_flat, w_proj).astype(jnp.bfloat16), 'tensor')  23.8 us
  transfers between devices with their start and end apart: 7, of which 6 were waited for; matrix products, arithmetic and copies ran while one was open for 6% of the time, Pallas kernels for 0%

commit v1 on v0

--- a/solution.py
+++ b/solution.py
@@ -14,6 +14,18 @@
 step_count = 2.0
 root_half = 0.7071067811865476
 normal_peak = 0.3989422804014327
+
+
+def collect(x, axis, dim):
+    ways, here = (lax.axis_size(axis), lax.axis_index(axis))
+    grown, reach = (x, 1)
+    while reach < ways:
+        theirs = lax.ppermute(grown, axis, [(d, d ^ reach) for d in range(ways)])
+        mine_first = jnp.concatenate([grown, theirs], axis=dim)
+        theirs_first = jnp.concatenate([theirs, grown], axis=dim)
+        grown = jnp.where(here & reach == 0, mine_first, theirs_first)
+        reach = 2 * reach
+    return grown
 
 
 def matmul(left_op, right_op):
@@ -131,7 +143,7 @@
     seq_count, seq_len, width = tokens.shape
     row_count = seq_count * seq_len
     in_full, out_full = (
-        lax.all_gather(in_weight.astype(jnp.bfloat16), "dp", axis=1, tiled=True),
+        collect(in_weight.astype(jnp.bfloat16), "dp", 1),
         lax.all_gather(out_weight.astype(jnp.bfloat16), "dp", axis=2, tiled=True),
     )
     group_width = in_full.shape[2]

time: 595 us -> 575 us (0.966)
  local copies, waits for them, and re-layouts: 43.2 us -> 26.5 us
  waiting for transfers between devices: 423 us -> 411 us
  starting transfers between devices: 0.47 us -> 7.95 us
    ppermute x0 -> x3, waiting for transfers between devices: none -> 94.3 us  [collect(): theirs = lax.ppermute(grown, axis, [(d, d ^ reach) for d in range(ways)])]
    all_gather x1, waiting for transfers between devices: 62.3 us -> 4.27 us  [local(): lax.all_gather(out_weight.astype(jnp.bfloat16), 'dp', axis=2, tiled=True)]
    all_gather x1 -> x0, waiting for transfers between devices: 57.4 us -> none  [local(): lax.all_gather(in_weight.astype(jnp.bfloat16), 'dp', axis=1, tiled=True)]
    ppermute x0 -> x3, starting transfers between devices: none -> 7.52 us  [collect(): theirs = lax.ppermute(grown, axis, [(d, d ^ reach) for d in range(ways)])]
    psum x1, waiting for transfers between devices: 23.8 us -> 30.9 us  [local(): lax.psum(matmul(mixed_flat, w_proj).astype(jnp.bfloat16), 'tensor')]
    unnamed x126 -> x114, local copies, waits for them, and re-layouts: 24.5 us -> 17.7 us
    slice x1 -> x0, local copies, waits for them, and re-layouts: 6.14 us -> none  [local(): w_query, w_key, w_value = (in_full[0], in_full[1], in_full[2])]
  transfers between devices with their start and end apart: 7 -> 9, of which waited for: 6 -> 8; matrix products, arithmetic and copies ran while one was open for 6% -> 6% of each run, Pallas kernels for 0% -> 0%
where the time goes in v1:
time: 575 us
  waiting for transfers between devices  411 us (71%)
  matrix products  42.7 us (7%)
  blocking collectives  37.4 us (7%)
  other arithmetic  34 us (6%)
  local copies, waits for them, and re-layouts  26.5 us (5%)
  between operations  15.5 us (3%)
  starting transfers between devices  7.95 us (1%)
    psum x1, waiting for transfers between devices, local(): lax.psum((grad_in, grad_outw, grad_bias, grad_norm), 'dp')  217 us
    ppermute x3, waiting for transfers between devices, collect(): theirs = lax.ppermute(grown, axis, [(d, d ^ reach) for d in range(ways)])  94.3 us
    psum x1, blocking collectives, local(): lax.psum((grad_in, grad_outw, grad_bias, grad_norm), 'dp')  37.4 us
    psum x1, waiting for transfers between devices, local(): lax.psum(ffn_part.astype(jnp.bfloat16), 'tensor').astype(jnp.float32)  35 us
    psum x1, waiting for transfers between devices, local(): lax.psum(matmul(mixed_flat, w_proj).astype(jnp.bfloat16), 'tensor')  30.9 us
    psum x1, waiting for transfers between devices, local(): lax.psum(back_part.astype(jnp.bfloat16), 'tensor').astype(jnp.float32)  29.2 us
    unnamed x114, local copies, waits for them, and re-layouts  17.7 us
  transfers between devices with their start and end apart: 9, of which 8 were waited for; matrix products, arithmetic and copies ran while one was open for 6% of the time, Pallas kernels for 0%

profile of v1, /device:TPU:0, one launch (start us, length us, event | category | flops | bytes accessed | tf_op | source)
XLA Modules:
  0.0 574.6 jit_solution(1039921530417711140)
XLA Ops:
  7.2 1.4 copy.102
  8.7 3.1 collective-permute-start
  11.7 8.1 %collective-permute-done = bf16[7,96,192]{1,2,0:T(8,128)(2,1)S(1)} collective-permute-done((bf16[7,96,192]{1,2,0:T(8,128)(2,1)S(1)}, bf16[7,96,192]{1,2,0:T(8,128)(2,1)S(1)}, u32[]{:S(2)}, u32[]{:S(2)}) %collective-permute-start) | collective-permute-done | bytes 258080 | tf_op jit(solution)/shard_map/ppermute | solution.py:23
  20.4 1.9 collective-permute-start.1
  22.3 14.9 %collective-permute-done.1 = bf16[7,192,192]{1,2,0:T(8,128)(2,1)} collective-permute-done((bf16[7,192,192]{1,2,0:T(8,128)(2,1)S(1)}, bf16[7,192,192]{1,2,0:T(8,128)(2,1)}, u32[]{:S(2)}, u32[]{:S(2)}) %collective-permute-start.1) | collective-permute-done | bytes 516128 | tf_op jit(solution)/shard_map/ppermute | solution.py:23
  37.2 2.1 maximum_select_fusion.1
  39.3 2.6 collective-permute-start.2
  43.8 71.3 %collective-permute-done.2 = bf16[7,384,192]{1,2,0:T(8,128)(2,1)S(1)} collective-permute-done((bf16[7,384,192]{1,2,0:T(8,128)(2,1)S(1)}, bf16[7,384,192]{1,2,0:T(8,128)(2,1)S(1)}, u32[]{:S(2)}, u32[]{:S(2)}) %collective-permute-start.2) | collective-permute-done | bytes 1032224 | tf_op jit(solution)/shard_map/ppermute | solution.py:23
  119.8 4.3 all-gather.2.cloned.1.call-done
  124.1 2.4 slice.97
  127.0 1.3 convolution_convert_fusion
  128.5 2.8 slice.99
  131.2 2.1 copy.128
  133.4 30.9 %all-reduce.8.cloned.1.call-done = bf16[512,768]{1,0:T(8,128)(2,1)} async-done(((bf16[512,768]{1,0:T(8,128)(2,1)}), bf16[512,768]{1,0:T(8,128)(2,1)}) %all-reduce.8.cloned.1.call-update) | async-done | bytes 786448 | tf_op jit(solution)/shard_map/psum | solution.py:169
  164.3 1.6 fusion.32
  167.4 1.1 copy-done.23
  169.3 1.7 bitcast_convert_fusion.1
  171.2 35.0 %all-reduce.10.cloned.1.call-done = bf16[512,768]{1,0:T(8,128)(2,1)} async-done(((bf16[512,768]{1,0:T(8,128)(2,1)}), bf16[512,768]{1,0:T(8,128)(2,1)}) %all-reduce.10.cloned.1.call-update) | async-done | bytes 786448 | tf_op jit(solution)/shard_map/psum | solution.py:181
  206.2 1.9 fusion.91
  210.2 1.6 fusion.23
  212.1 2.0 fusion.100
  215.0 1.7 bitcast_convert_fusion
  216.8 3.4 fusion.41
  220.2 2.5 convolution_bitcast_fusion
  222.8 29.2 %all-reduce.12.cloned.1.call-done = bf16[512,768]{1,0:T(8,128)(2,1)} async-done(((bf16[512,768]{1,0:T(8,128)(2,1)}), bf16[512,768]{1,0:T(8,128)(2,1)}) %all-reduce.12.cloned.1.call-update) | async-done | bytes 786448 | tf_op jit(solution)/shard_map/psum | solution.py:198
  251.9 2.9 multiply_reduce_fusion.1
  254.9 1.4 fusion.90
  257.2 2.3 fusion.101
  259.5 7.2 %fusion.93 = (f32[3,64]{1,0:T(4,128)}, bf16[512,3,64]{0,2,1:T(8,128)(2,1)S(1)}) fusion(bf16[512,3,64]{0,2,1:T(8,128)(2,1)S(1)} %bitcast.224, f32[3,512,512]{1,2,0:T(8,128)} %fusion.101, f32[3,512]{1,0:T(4,128)S(1)} %log_add_fusion, f32[3,512,512]{1,2,0:T(8,128)} %copy-done.5, pred[512]{0:T(512)(128)(4,1)S(1)} %iota_compare_fusion), kind=kOutput, calls=%fused_computation.164 | convolution fusion | flops 109512512 | bytes 6692096 | tf_op jit(solution)/shard_map/while/body/eval_jaxpr/hqk,khe->qhe/dot_general | solution.py:109
  266.7 6.6 %fusion.35 = bf16[3,64,512]{2,1,0:T(8,128)(2,1)S(1)} fusion(bf16[512,3,64]{0,2,1:T(8,128)(2,1)S(1)} %bitcast.234, f32[3,512,512]{1,2,0:T(8,128)} %fusion.101, f32[3,512,512]{1,2,0:T(8,128)} %copy-done.5, f32[3,512]{1,0:T(4,128)S(1)} %log_add_fusion, pred[512]{0:T(512)(128)(4,1)S(1)} %iota_compare_fusion), kind=kOutput, calls=%fused_computation.66 | convolution fusion | flops 109414400 | bytes 6691328 | tf_op jit(solution)/shard_map/while/body/eval_jaxpr/hqk,qhe->khe/dot_general | solution.py:112
  273.3 3.6 fusion.94
  278.1 1.2 convolution_bitcast_fusion.4
  279.3 1.1 convolution_bitcast_fusion.1
  281.6 1.4 add_convert_fusion.1
  283.1 3.9 pad_maximum_fusion.1
  287.0 2.2 pad_maximum_fusion
  289.2 2.3 fusion.92
  291.6 1.5 copy.129
  294.6 37.4 %all-reduce = (f32[6,192]{1,0:T(8,128)S(1)}, f32[6,768]{1,0:T(8,128)S(1)}) all-reduce(f32[6,192]{1,0:T(8,128)S(1)} %pad_maximum_fusion.6, f32[6,768]{1,0:T(8,128)S(1)} %stack.83), channel_id=1, replica_groups=mesh['dp'=8,'tensor'=4] {'dp'}, use_global_device_ids=true, to_apply=%region_20.21 | all-reduce | flops 5760 | bytes 46080 | tf_op jit(solution)/shard_map/psum | solution.py:253
  334.5 2.2 fusion.39
  336.7 217.0 %all-reduce.16.cloned.1.call-done = (f32[7,768,192]{1,2,0:T(8,128)}, f32[5,192,768]{2,1,0:T(8,128)}) async-done(((f32[7,768,192]{1,2,0:T(8,128)}, f32[5,192,768]{2,1,0:T(8,128)}), (f32[7,768,192]{1,2,0:T(8,128)}, f32[5,192,768]{2,1,0:T(8,128)})) %all-reduce.16.cloned.1.call-update) | async-done | bytes 7077904 | tf_op jit(solution)/shard_map/psum | solution.py:253
  553.7 1.7 fusion.64
  555.3 1.1 copy.118
  556.5 2.7 fusion.68
  559.2 2.4 copy.119
  561.5 2.2 fusion.69
  563.7 1.3 fusion.70
  565.2 1.6 copy.120
  (174 shorter events, 21.3 us)
Async XLA Ops:
  7.2 116.9 %all-gather.2.cloned.1.call-start = ((), (), s32[]{:S(2)}) async-start(), calls=%async_computation | async-start | bytes 3538944 | tf_op jit(solution)/shard_map/all_gather | solution.py:147
  8.6 30.7 %copy-start.9 = (f32[7,96,192]{1,2,0:T(8,128)}, f32[7,96,192]{1,2,0:T(8,128)S(1)}, u32[]{:S(2)}) copy-start(f32[7,96,192]{1,2,0:T(8,128)S(1)} %copy.102) | copy-start | bytes 1548292
  8.7 11.1 %collective-permute-start = (bf16[7,96,192]{1,2,0:T(8,128)(2,1)S(1)}, bf16[7,96,192]{1,2,0:T(8,128)(2,1)S(1)}, u32[]{:S(2)}, u32[]{:S(2)}) collective-permute-start(bf16[7,96,192]{1,2,0:T(8,128)(2,1)S(1)} %convert_element_type.132), channel_id=1, source_target_pairs={{0,4},{4,0},{8,12},{12,8},{16,20},{20,16},{24,28},{28,24},{1,5},{5... | collective-permute-start | bytes 774152 | tf_op jit(solution)/shard_map/ppermute | solution.py:23
  11.7 30.1 %copy-start.18 = (f32[5,192,96]{2,1,0:T(8,128)S(1)}, f32[5,192,96]{2,1,0:T(8,128)}, u32[]{:S(2)}) copy-start(f32[5,192,96]{2,1,0:T(8,128)} %param.15) | copy-start | bytes 1105924
  20.4 16.8 %collective-permute-start.1 = (bf16[7,192,192]{1,2,0:T(8,128)(2,1)S(1)}, bf16[7,192,192]{1,2,0:T(8,128)(2,1)}, u32[]{:S(2)}, u32[]{:S(2)}) collective-permute-start(bf16[7,192,192]{1,2,0:T(8,128)(2,1)S(1)} %maximum_select_fusion.2), channel_id=1, source_target_pairs={{0,8},{4,12},{8,0},{12,4},{16,24},{20,28},{24,16},{28,20},{1,9},{5... | collective-permute-start | bytes 1548296 | tf_op jit(solution)/shard_map/ppermute | solution.py:23
  22.3 21.5 %copy-start.39 = (f32[6,192]{1,0:T(8,128)S(1)}, f32[6,192]{1,0:T(8,128)}, u32[]{:S(2)}) copy-start(f32[6,192]{1,0:T(8,128)} %param.16) | copy-start | bytes 13828
  39.3 75.8 %collective-permute-start.2 = (bf16[7,384,192]{1,2,0:T(8,128)(2,1)S(1)}, bf16[7,384,192]{1,2,0:T(8,128)(2,1)S(1)}, u32[]{:S(2)}, u32[]{:S(2)}) collective-permute-start(bf16[7,384,192]{1,2,0:T(8,128)(2,1)S(1)} %maximum_select_fusion.1), channel_id=1, source_target_pairs={{0,16},{4,20},{8,24},{12,28},{16,0},{20,4},{24,8},{28,12},{1,17},{... | collective-permute-start | bytes 3096584 | tf_op jit(solution)/shard_map/ppermute | solution.py:23
  43.0 121.3 %all-reduce.8.cloned.1.call-start = ((), (), s32[]{:S(2)}) async-start(), calls=%async_computation.1 | async-start | bytes 1572864 | tf_op jit(solution)/shard_map/psum | solution.py:169
  43.7 71.8 %copy-start = (bf16[1,512,768]{2,1,0:T(8,128)(2,1)S(1)}, bf16[1,512,768]{2,1,0:T(8,128)(2,1)}, u32[]{:S(2)}) copy-start(bf16[1,512,768]{2,1,0:T(8,128)(2,1)} %param.11) | copy-start | bytes 2359300
  115.6 2.4 copy-start.6
  119.8 8.5 %copy-start.27 = (bf16[3,64,512]{2,1,0:T(8,128)(2,1)}, bf16[3,64,512]{2,1,0:T(8,128)(2,1)S(1)}, u32[]{:S(2)}) copy-start(bf16[3,64,512]{2,1,0:T(8,128)(2,1)S(1)} %convolution_convert_fusion.1) | copy-start | bytes 589828
  126.5 1.9 copy-start.36
  128.3 77.9 %all-reduce.10.cloned.1.call-start = ((), (), s32[]{:S(2)}) async-start(), calls=%async_computation.2 | async-start | bytes 1572864 | tf_op jit(solution)/shard_map/psum | solution.py:181
  164.3 2.1 slice-start
  167.4 1.8 copy-start.25
  169.3 1.7 copy-start.11
  171.0 80.9 %all-reduce.12.cloned.1.call-start = ((), (), s32[]{:S(2)}) async-start(), calls=%async_computation.3 | async-start | bytes 1572864 | tf_op jit(solution)/shard_map/psum | solution.py:198
  210.1 2.0 copy-start.26
  211.7 2.4 copy-start.1
  212.1 2.9 copy-start.7
  215.0 1.8 copy-start.2
  216.7 117.7 %all-reduce.14.cloned.1.call-start = ((), (), s32[]{:S(2)}) async-start(), calls=%async_computation.4 | async-start | bytes 1572864 | tf_op jit(solution)/shard_map/psum | solution.py:225
  216.8 3.4 copy-start.51
  251.9 2.9 copy-start.3
  251.9 2.9 copy-start.12
  257.2 2.3 copy-start.30
  259.5 7.2 %copy-start.35 = (bf16[192,512]{1,0:T(8,128)(2,1)S(1)}, bf16[192,512]{1,0:T(8,128)(2,1)}, u32[]{:S(2)}) copy-start(bf16[192,512]{1,0:T(8,128)(2,1)} %copy-done.34) | copy-start | bytes 589828
  266.7 11.0 %copy-start.31 = (bf16[512,3,64]{0,2,1:T(8,128)(2,1)}, bf16[512,3,64]{0,2,1:T(8,128)(2,1)S(1)}, u32[]{:S(2)}) copy-start(bf16[512,3,64]{0,2,1:T(8,128)(2,1)S(1)} %get-tuple-element.171) | copy-start | bytes 589828
  273.3 3.6 copy-start.8
  277.7 1.7 copy-start.28
  283.0 4.0 copy-start.15
  283.0 270.6 %all-reduce.16.cloned.1.call-start = ((), (), s32[]{:S(2)}) async-start(), calls=%async_computation.5 | async-start | bytes 14155776 | tf_op jit(solution)/shard_map/psum | solution.py:253
  283.1 3.9 copy-start.16
  291.5 2.7 copy-start.45
  291.5 2.7 copy-start.38
  291.5 2.8 copy-start.49
  291.5 2.9 copy-start.48
  291.5 2.9 copy-start.44
  291.5 2.9 copy-start.43
  291.5 2.9 copy-start.42
  291.6 2.9 copy-start.41
  291.6 3.0 copy-start.47
  291.6 41.6 %copy-start.37 = (f32[6,768]{1,0:T(8,128)S(1)}, f32[6,768]{1,0:T(8,128)}, u32[]{:S(2)}) copy-start(f32[6,768]{1,0:T(8,128)} %param.17) | copy-start | bytes 55300
  331.9 4.7 copy-start.40
  332.0 4.7 copy-start.46
  553.6 2.8 copy-start.10
  559.1 2.4 copy-start.17
  559.1 4.5 copy-start.19
  (14 other events, 18.4 us)
Sparse Core Ops, SparseCore 0:
  43.1 80.9 all-gather.1
  128.5 35.7 all-reduce.7
  171.1 35.0 all-reduce.9
  216.9 35.0 all-reduce.11
  283.1 35.0 all-reduce.13
  322.1 231.5 all-reduce.15
